TPU v7x, 32 devices: a whole 2x2x4 slice. The times are simulated.
32 devices in a mesh: dp: 16 (over z, y, x), tensor: 2 (over core).
Axes of the slice: x: 2, y: 2, z: 4, core: 2. Of those that a mesh axis runs over, the one named last changes fastest.
Arguments:
- inputs: bfloat16 [16, 1024, 768], P(None, 'dp', 'tensor'), may hold values from -6 to 6
- lengths: int32 [16], replicated, may hold values from 1 to 1024, 12288 in all
- order: int32 [16], replicated, may hold values from 0 to 15, each once
- w_query: bfloat16 [768, 768], P(None, 'tensor'), may hold values from -0.3125 to 0.3125
- b_query: bfloat16 [768], P('tensor'), may hold values from -3 to 3
- w_key: bfloat16 [768, 768], P(None, 'tensor'), may hold values from -0.3125 to 0.3125
- w_value: bfloat16 [768, 768], P(None, 'tensor'), may hold values from -0.21875 to 0.21875
- b_value: bfloat16 [768], P('tensor'), may hold values from -3 to 3
- w_out: bfloat16 [768, 768], P('tensor'), may hold values from -0.875 to 0.875
- b_out: bfloat16 [768], P('tensor'), may hold values from -3 to 3
- gain_one: bfloat16 [768], P('tensor'), may hold values from 0.5 to 1.5
- shift_one: bfloat16 [768], P('tensor'), may hold values from -3 to 3
- w_up: bfloat16 [768, 3072], P(None, 'tensor'), may hold values from -0.21875 to 0.21875
- b_up: bfloat16 [3072], P('tensor'), may hold values from -3 to 3
- w_down: bfloat16 [3072, 768], P('tensor'), may hold values from -0.109375 to 0.109375
- b_down: bfloat16 [768], P('tensor'), may hold values from -3 to 3
- gain_two: bfloat16 [768], P('tensor'), may hold values from 0.5 to 1.5
- shift_two: bfloat16 [768], P('tensor'), may hold values from -3 to 3
- cotangent: bfloat16 [16, 1024, 768], P('dp', 'tensor'), may hold values from -6 to 6
Outputs:
- output: bfloat16 [16, 1024, 768], P('dp', 'tensor')
- input_grad: bfloat16 [16, 1024, 768], P(None, 'dp', 'tensor')
- grad_w_query: float32 [768, 768], P(None, 'tensor')
- grad_b_query: float32 [768], P('tensor')
- grad_w_key: float32 [768, 768], P(None, 'tensor')
- grad_w_value: float32 [768, 768], P(None, 'tensor')
- grad_b_value: float32 [768], P('tensor')
- grad_w_out: float32 [768, 768], P('tensor')
- grad_b_out: float32 [768], P('tensor')
- grad_gain_one: float32 [768], P('tensor')
- grad_shift_one: float32 [768], P('tensor')
- grad_w_up: float32 [768, 3072], P(None, 'tensor')
- grad_b_up: float32 [3072], P('tensor')
- grad_w_down: float32 [3072, 768], P('tensor')
- grad_b_down: float32 [768], P('tensor')
- grad_gain_two: float32 [768], P('tensor')
- grad_shift_two: float32 [768], P('tensor')
Inputs may be any that keep to these rules, and one draw needn't show every extreme that they name: Valid tokens of each sequence; the first lengths entries of a sequence's 1024 slots hold its tokens, and some sequence fills all 1024. `order`: a permutation of the 16 sequences.
All inputs are finite; a program needn't handle non-finite values.
Results may differ from a plain program's by a relative error of at most 0.015.
The roundings to bfloat16 on the way count: a program that leaves them out, or rounds other values in their place, can miss the bound.
Values may be sent and summed in bfloat16 or wider, within the bound.
No kernel may reach another device: no remote copies, remote signals or barrier semaphores. Data moves between devices by JAX's collectives and lax.ppermute only.
A program may use at most 192 MiB of HBM per device.

v0:
```python
import jax
import jax.numpy as jnp
from jax import lax
from jax.sharding import PartitionSpec as P

HEAD_DIM = 64
epsilon = 1e-06
masked_score = -1e30


def layer_norm(value, gain, shift):
    center = value - jnp.mean(value, axis=-1, keepdims=True)
    spread = jnp.mean(center * center, axis=-1, keepdims=True)
    return center * lax.rsqrt(spread + epsilon) * gain + shift


def gelu_exact(value):
    return jax.nn.gelu(value, approximate=False)


def product(left, right, form):
    return jnp.einsum(form, left, right, preferred_element_type=jnp.float32)


def masked_scores(query, keys, length):
    span = query.shape[0]
    scores = product(query, keys, "qhd,khd->hqk") * query.shape[-1] ** (-0.5)
    valid = jnp.arange(span) < length
    return jnp.where(valid[None, None, :], scores, masked_score)


def attend_forward(packed):
    query, keys, values, length = packed
    scores = masked_scores(query, keys, length)
    top = jnp.max(scores, axis=-1, keepdims=True)
    weights = jnp.exp(scores - top)
    total = jnp.sum(weights, axis=-1, keepdims=True)
    probs_low = (weights / total).astype(jnp.bfloat16)
    mixed = product(probs_low, values, "hqk,khd->qhd")
    return (mixed, (top + jnp.log(total))[..., 0])


def attend_backward(packed):
    query, keys, values, length, log_total, grad_mixed = packed
    scale = query.shape[-1] ** (-0.5)
    scores = masked_scores(query, keys, length)
    probs = jnp.exp(scores - log_total[..., None])
    grad_values = product(probs.astype(jnp.bfloat16), grad_mixed, "hqk,qhd->khd")
    grad_probs = product(grad_mixed, values, "qhd,khd->hqk")
    inner = jnp.sum(grad_probs * probs, axis=-1, keepdims=True)
    grad_scores = (probs * (grad_probs - inner) * scale).astype(jnp.bfloat16)
    grad_query = product(grad_scores, keys, "hqk,khd->qhd")
    grad_keys = product(grad_scores, query, "hqk,qhd->khd")
    return (grad_query, grad_keys, grad_values)


def on_device(
    inputs,
    lengths,
    order,
    w_query,
    b_query,
    w_key,
    w_value,
    b_value,
    w_out,
    b_out,
    gain_one,
    shift_one,
    w_up,
    b_up,
    w_down,
    b_down,
    gain_two,
    shift_two,
    cotangent,
):
    dp_count = lax.axis_size("dp")
    seq_local = inputs.shape[0] // dp_count
    seq_len = inputs.shape[1] * dp_count
    half = seq_len // lax.axis_size("tensor")
    offset = lax.axis_index("tensor") * half
    width = w_query.shape[0]
    local_width = w_query.shape[1]
    local_heads = local_width // HEAD_DIM
    token_count = seq_local * seq_len
    head_shape = (seq_local, seq_len, local_heads, HEAD_DIM)
    factor = (order.shape[0] * seq_len) ** (-0.5)
    arranged = inputs[order]
    vectors = jnp.stack([b_out, gain_one, shift_one, b_down, gain_two, shift_two])[None]
    dealt_half = lax.all_to_all(arranged, "dp", split_axis=0, concat_axis=1, tiled=True)
    dealt, vectors_full = (
        lax.all_gather(dealt_half, "tensor", axis=2, tiled=True),
        lax.all_gather(vectors, "tensor", axis=2, tiled=True),
    )
    vectors_full = vectors_full[0].astype(jnp.float32)
    bias_out = vectors_full[0]
    gain_first = vectors_full[1]
    shift_first = vectors_full[2]
    bias_down = vectors_full[3]
    gain_second = vectors_full[4]
    shift_second = vectors_full[5]
    dealt_lengths = lax.dynamic_slice_in_dim(
        lengths[order], lax.axis_index("dp") * seq_local, seq_local
    )
    tokens_flat = dealt.reshape(token_count, width)
    query = (product(tokens_flat, w_query, "nd,df->nf") + b_query.astype(jnp.float32)).astype(
        jnp.bfloat16
    )
    keys = product(tokens_flat, w_key, "nd,df->nf").astype(jnp.bfloat16)
    values = (product(tokens_flat, w_value, "nd,df->nf") + b_value.astype(jnp.float32)).astype(
        jnp.bfloat16
    )
    query_heads = query.reshape(head_shape)
    key_heads = keys.reshape(head_shape)
    value_heads = values.reshape(head_shape)
    mixed, log_total = lax.map(attend_forward, (query_heads, key_heads, value_heads, dealt_lengths))
    mixed = mixed.astype(jnp.bfloat16).reshape(token_count, local_width)
    attention = product(mixed, w_out, "nh,hd->nd").reshape(seq_local, seq_len, width)
    attention = lax.psum_scatter(attention, "tensor", scatter_dimension=1, tiled=True)
    residual = lax.dynamic_slice_in_dim(dealt, offset, half, 1).astype(jnp.float32)
    normed, norm_one_back = jax.vjp(
        layer_norm, residual + attention + bias_out, gain_first, shift_first
    )
    normed_low = normed.astype(jnp.bfloat16)
    normed_all = lax.all_gather(normed_low, "tensor", axis=1, tiled=True)
    normed_rows = normed_all.reshape(token_count, width)
    upper = product(normed_rows, w_up, "nd,df->nf") + b_up.astype(jnp.float32)
    active, gelu_back = jax.vjp(gelu_exact, upper)
    active_low = active.astype(jnp.bfloat16)
    feed_terms = product(active_low, w_down, "nf,fd->nd").reshape(seq_local, seq_len, width)
    feed = lax.psum_scatter(feed_terms, "tensor", scatter_dimension=1, tiled=True)
    result, norm_two_back = jax.vjp(
        layer_norm, normed + feed + bias_down, gain_second, shift_second
    )
    output = result.astype(jnp.bfloat16)
    grad_two, grad_gain_two, grad_shift_two = norm_two_back(cotangent.astype(jnp.float32))
    grad_bias_down = jnp.sum(grad_two, axis=(0, 1))
    grad_two_low = grad_two.astype(jnp.bfloat16)
    grad_all = lax.all_gather(grad_two_low, "tensor", axis=1, tiled=True)
    grad_rows = grad_all.reshape(token_count, width)
    grad_active = product(grad_rows, w_down, "nd,fd->nf")
    (grad_upper,) = gelu_back(grad_active)
    grad_upper_low = grad_upper.astype(jnp.bfloat16)
    grad_w_up = product(normed_rows, grad_upper_low, "nd,nf->df")
    grad_b_up = jnp.sum(grad_upper, axis=0)
    grad_w_down = product(active_low, grad_rows, "nf,nd->fd")
    normed_terms = product(grad_upper_low, w_up, "nf,df->nd").reshape(seq_local, seq_len, width)
    grad_normed = lax.psum_scatter(normed_terms, "tensor", scatter_dimension=1, tiled=True)
    grad_one, grad_gain_one, grad_shift_one = norm_one_back(grad_normed + grad_two)
    grad_bias_out = jnp.sum(grad_one, axis=(0, 1))
    grad_one_all = lax.all_gather(
        grad_one.astype(jnp.bfloat16), "tensor", axis=1, tiled=True
    ).reshape(token_count, width)
    grad_w_out = product(mixed, grad_one_all, "nh,nd->hd")
    grad_mixed = product(grad_one_all, w_out, "nd,hd->nh").astype(jnp.bfloat16).reshape(head_shape)
    grad_query, grad_keys, grad_values = lax.map(
        attend_backward, (query_heads, key_heads, value_heads, dealt_lengths, log_total, grad_mixed)
    )
    grad_query = grad_query.astype(jnp.bfloat16).reshape(token_count, local_width)
    grad_keys = grad_keys.astype(jnp.bfloat16).reshape(token_count, local_width)
    grad_values = grad_values.astype(jnp.bfloat16).reshape(token_count, local_width)
    grad_w_query = product(tokens_flat, grad_query, "nd,nf->df")
    grad_b_query = jnp.sum(grad_query, axis=0, dtype=jnp.float32)
    grad_w_key = product(tokens_flat, grad_keys, "nd,nf->df")
    grad_w_value = product(tokens_flat, grad_values, "nd,nf->df")
    grad_b_value = jnp.sum(grad_values, axis=0, dtype=jnp.float32)
    grad_inputs = (
        product(grad_query, w_query, "nf,df->nd")
        + product(grad_keys, w_key, "nf,df->nd")
        + product(grad_values, w_value, "nf,df->nd")
    )
    grad_inputs = grad_inputs.reshape(seq_local, seq_len, width)
    own_rows = lax.dynamic_slice_in_dim(grad_inputs, offset, half, 1) + grad_one
    grad_inputs = lax.dynamic_update_slice_in_dim(grad_inputs, own_rows, offset, 1)
    vector_grads = jnp.stack(
        [
            grad_bias_out,
            grad_gain_one,
            grad_shift_one,
            grad_bias_down,
            grad_gain_two,
            grad_shift_two,
        ]
    )[None]
    grad_inputs, vector_grads = (
        lax.psum_scatter(
            grad_inputs.astype(jnp.bfloat16), "tensor", scatter_dimension=2, tiled=True
        ).astype(jnp.float32),
        lax.psum_scatter(
            vector_grads.astype(jnp.bfloat16), "tensor", scatter_dimension=2, tiled=True
        ).astype(jnp.float32),
    )
    returned = lax.all_to_all(
        grad_inputs.astype(jnp.bfloat16), "dp", split_axis=1, concat_axis=0, tiled=True
    )
    inverse = jnp.zeros_like(order).at[order].set(jnp.arange(order.shape[0], dtype=jnp.int32))
    input_grad = returned[inverse]
    summed = lax.psum(
        (
            grad_w_query,
            grad_b_query,
            grad_w_key,
            grad_w_value,
            grad_b_value,
            grad_w_out,
            grad_w_up,
            grad_b_up,
            grad_w_down,
            vector_grads,
        ),
        "dp",
    )
    vector_sums = summed[9][0] * factor
    return (
        output,
        input_grad,
        summed[0] * factor,
        summed[1] * factor,
        summed[2] * factor,
        summed[3] * factor,
        summed[4] * factor,
        summed[5] * factor,
        vector_sums[0],
        vector_sums[1],
        vector_sums[2],
        summed[6] * factor,
        summed[7] * factor,
        summed[8] * factor,
        vector_sums[3],
        vector_sums[4],
        vector_sums[5],
    )


def solution(mesh):
    return jax.shard_map(
        on_device,
        mesh=mesh,
        in_specs=(
            P(None, "dp", "tensor"),
            P(),
            P(),
            P(None, "tensor"),
            P("tensor"),
            P(None, "tensor"),
            P(None, "tensor"),
            P("tensor"),
            P("tensor", None),
            P("tensor"),
            P("tensor"),
            P("tensor"),
            P(None, "tensor"),
            P("tensor"),
            P("tensor", None),
            P("tensor"),
            P("tensor"),
            P("tensor"),
            P("dp", "tensor", None),
        ),
        out_specs=(
            P("dp", "tensor", None),
            P(None, "dp", "tensor"),
            P(None, "tensor"),
            P("tensor"),
            P(None, "tensor"),
            P(None, "tensor"),
            P("tensor"),
            P("tensor", None),
            P("tensor"),
            P("tensor"),
            P("tensor"),
            P(None, "tensor"),
            P("tensor"),
            P("tensor", None),
            P("tensor"),
            P("tensor"),
            P("tensor"),
        ),
        check_vma=False,
    )
```

profile of v0, /device:TPU:0, one launch (start us, length us, event | category | flops | bytes accessed | tf_op | source)
XLA Modules:
  0.0 789.3 jit_solution(8190659484800640758)
XLA Ops:
  10.5 29.5 %all_to_all.24 = bf16[16,64,384]{2,1,0:T(8,128)(2,1)} all-to-all(bf16[16,64,384]{2,1,0:T(8,128)(2,1)S(1)} %gather_fusion), channel_id=1, replica_groups=mesh['dp'=16,'tensor'=2] {'dp'}, dimensions={0} | all-to-all | bytes 1572864 | tf_op jit(solution)/shard_map/all_to_all | solution.py:91
  42.0 5.6 all-gather.6.cloned.1.call-done
  51.0 10.6 %fusion.3 = (f32[6,1024]{1,0:T(8,128)S(1)}, f32[6,1024,1024]{1,2,0:T(8,128)}) fusion(pred[1024]{0:T(1024)(128)(4,1)S(1)} %iota_compare_fusion, bf16[1024,6,64]{0,2,1:T(8,128)(2,1)S(1)} %bitcast.140, bf16[1024,6,64]{0,2,1:T(8,128)(2,1)S(1)} %bitcast.138), kind=kOutput, calls=%fused_computation.13 | convolution fusion | flops 824174592 | bytes 26764288 | tf_op jit(solution)/shard_map/while/body/eval_jaxpr/qhd,khd->hqk/dot_general | solution.py:22
  61.6 11.8 %fusion.2 = f32[6,1024]{1,0:T(8,128)S(1)} fusion(f32[6,1024,1024]{1,2,0:T(8,128)} %get-tuple-element.112, f32[6,1024]{1,0:T(8,128)S(1)} %get-tuple-element.111, pred[1024]{0:T(1024)(128)(4,1)S(1)} %iota_compare_fusion), kind=kLoop, calls=%fused_computation.12 | loop fusion | flops 25159680 | bytes 25216000 | tf_op jit(solution)/shard_map/while/body/eval_jaxpr/reduce_sum | solution.py:37
  74.3 11.8 %fusion.91 = bf16[6,64,1024]{2,1,0:T(8,128)(2,1)S(1)} fusion(bf16[1024,6,64]{0,2,1:T(8,128)(2,1)S(1)} %bitcast.134, f32[6,1024,1024]{1,2,0:T(8,128)} %get-tuple-element.112, f32[6,1024]{1,0:T(8,128)S(1)} %fusion.2, f32[6,1024]{1,0:T(8,128)S(1)} %get-tuple-element.111, pred[1024]{0:T(1024)(128)(4,1)S(1)} %iota_compare_fusion), kind=kOutput, calls=%fused_computation.106 | convolution fusion | flops 837156864 | bytes 26788864 | tf_op jit(solution)/shard_map/while/body/eval_jaxpr/hqk,khd->qhd/dot_general | solution.py:22
  92.1 10.2 %reduce-scatter.10.cloned.1.call-done = f32[1,512,768]{2,1,0:T(8,128)} async-done(((f32[1,1024,768]{2,1,0:T(8,128)}), f32[1,512,768]{2,1,0:T(8,128)}) %reduce-scatter.10.cloned.1.call-update) | async-done | bytes 1572880 | tf_op jit(solution)/shard_map/reduce_scatter | solution.py:120
  106.6 11.2 %all-gather.8.cloned.1.call-done = bf16[1,1024,768]{2,1,0:T(8,128)(2,1)} async-done(((bf16[1,512,768]{2,1,0:T(8,128)(2,1)}), bf16[1,1024,768]{2,1,0:T(8,128)(2,1)}) %all-gather.8.cloned.1.call-update) | async-done | bytes 1572880 | tf_op jit(solution)/shard_map/all_gather | solution.py:126
  117.7 18.2 %multiply_convert_fusion.1 = (bf16[1024,1536]{1,0:T(8,128)(2,1)S(1)}, f32[1024,1536]{1,0:T(8,128)}, f32[1024,1536]{1,0:T(8,128)}) fusion(f32[1536]{0:T(1024)S(1)} %convert_element_type.127, bf16[768,1536]{1,0:T(8,128)(2,1)S(1)} %copy-done, bf16[1,1024,768]{2,1,0:T(8,128)(2,1)} %all-gather.8.cloned.1.call-done), kind=kOutput, calls=%fused_computation.31 | convolution fusion | flops 2519728128 | bytes 19666944 | tf_op jit(solution)/shard_map/nd,df->nf/dot_general | solution.py:22
  137.6 4.3 convolution_bitcast_fusion.1
  141.9 12.4 %reduce-scatter.12.cloned.1.call-done = f32[1,512,768]{2,1,0:T(8,128)} async-done(((f32[1,1024,768]{2,1,0:T(8,128)}), f32[1,512,768]{2,1,0:T(8,128)}) %reduce-scatter.12.cloned.1.call-update) | async-done | bytes 1572880 | tf_op jit(solution)/shard_map/reduce_scatter | solution.py:132
  162.3 10.8 %all-gather.10.cloned.1.call-done = bf16[1,1024,768]{2,1,0:T(8,128)(2,1)} async-done(((bf16[1,512,768]{2,1,0:T(8,128)(2,1)}), bf16[1,1024,768]{2,1,0:T(8,128)(2,1)}) %all-gather.10.cloned.1.call-update) | async-done | bytes 1572880 | tf_op jit(solution)/shard_map/all_gather | solution.py:140
  173.1 10.2 %fusion.118 = (f32[1536]{0:T(1024)S(1)}, bf16[1024,1536]{1,0:T(8,128)(2,1)S(1)}) fusion(f32[1024,1536]{1,0:T(8,128)} %get-tuple-element.103, bf16[1536,768]{1,0:T(8,128)(2,1)} %param.33, bf16[1,1024,768]{2,1,0:T(8,128)(2,1)} %all-gather.10.cloned.1.call-done, f32[1024,1536]{1,0:T(8,128)} %get-tuple-element.113, f32[1536]{0:T(1024)S(1)} %convert_element_type.127), kind=kOutput, calls=%fused_computation.168 | convolution fusion | flops 2441083392 | bytes 19673088 | tf_op jit(solution)/shard_map/nd,fd->nf/dot_general | solution.py:22
  184.9 4.3 convolution_bitcast_fusion
  189.3 12.4 %reduce-scatter.14.cloned.1.call-done = f32[1,512,768]{2,1,0:T(8,128)} async-done(((f32[1,1024,768]{2,1,0:T(8,128)}), f32[1,512,768]{2,1,0:T(8,128)}) %reduce-scatter.14.cloned.1.call-update) | async-done | bytes 1572880 | tf_op jit(solution)/shard_map/reduce_scatter | solution.py:149
  207.4 11.2 %all-gather.12.cloned.1.call-done = bf16[1,1024,768]{2,1,0:T(8,128)(2,1)} async-done(((bf16[1,512,768]{2,1,0:T(8,128)(2,1)}), bf16[1,1024,768]{2,1,0:T(8,128)(2,1)}) %all-gather.12.cloned.1.call-update) | async-done | bytes 1572880 | tf_op jit(solution)/shard_map/all_gather | solution.py:152
  220.8 10.2 %fusion.119 = f32[6,1024,1024]{1,2,0:T(8,128)} fusion(bf16[1024,6,64]{0,2,1:T(8,128)(2,1)S(1)} %bitcast.136, bf16[1024,6,64]{0,2,1:T(8,128)(2,1)S(1)} %bitcast.135), kind=kOutput, calls=%fused_computation.169 | convolution fusion | flops 805306368 | bytes 26738688 | tf_op jit(solution)/shard_map/while/body/eval_jaxpr/qhd,khd->hqk/dot_general | solution.py:22
  231.1 12.3 %convert_reduce_fusion = (f32[6,64]{1,0:T(8,128)S(1)}, bf16[6,64,1024]{2,1,0:T(8,128)(2,1)}) fusion(bf16[1024,6,64]{0,2,1:T(8,128)(2,1)S(1)} %bitcast.137, f32[6,1024,1024]{1,2,0:T(8,128)} %get-tuple-element.112, f32[6,1024]{1,0:T(8,128)S(1)} %log_add_fusion, pred[1024]{0:T(1024)(128)(4,1)S(1)} %iota_compare_fusion), kind=kOutput, calls=%fused_computation.88 | convolution fusion | flops 831651456 | bytes 26765824 | tf_op jit(solution)/shard_map/while/body/eval_jaxpr/hqk,qhd->khd/dot_general | solution.py:22
  243.4 34.1 %fusion.88 = bf16[6,64,1024]{2,1,0:T(8,128)(2,1)S(1)} fusion(bf16[1024,6,64]{0,2,1:T(8,128)(2,1)S(1)} %bitcast.141, f32[6,1024,1024]{1,2,0:T(8,128)} %fusion.119, f32[6,1024,1024]{1,2,0:T(8,128)} %get-tuple-element.112, f32[6,1024]{1,0:T(8,128)S(1)} %log_add_fusion, pred[1024]{0:T(1024)(128)(4,1)S(1)} %iota_compare_fusion), kind=kOutput, calls=%fused_computation.105 | convolution fusion | flops 874912768 | bytes 51930112 | tf_op jit(solution)/shard_map/while/body/eval_jaxpr/hqk,qhd->khd/dot_general | solution.py:22
  277.6 34.3 %convert_reduce_fusion.1 = (f32[6,64]{1,0:T(8,128)S(1)}, bf16[6,64,1024]{2,1,0:T(8,128)(2,1)S(1)}) fusion(bf16[1024,6,64]{0,2,1:T(8,128)(2,1)S(1)} %bitcast.139, f32[6,1024,1024]{1,2,0:T(8,128)} %fusion.119, f32[6,1024,1024]{1,2,0:T(8,128)} %get-tuple-element.112, f32[6,1024]{1,0:T(8,128)S(1)} %log_add_fusion, pred[1024]{0:T(1024)(128)(4,1)S(1)} %iota_compare_fusion), kind=kOutput, calls=%fused_computation.89 | convolution fusion | flops 875698816 | bytes 51931648 | tf_op jit(solution)/shard_map/while/body/eval_jaxpr/hqk,khd->qhd/dot_general | solution.py:22
  318.5 5.6 copy.58
  324.1 3.6 copy.68
  328.0 7.4 fusion.48
  335.4 4.3 fusion.54
  341.3 3.2 fusion.44
  344.5 3.6 fusion.58
  352.2 3.1 reshape_bitcast_fusion
  355.3 5.0 copy.53
  360.9 5.4 reduce.43
  367.4 6.8 all-to-all-start.1
  376.3 98.0 %all-reduce = (f32[384]{0:T(512)S(1)}, f32[384]{0:T(512)S(1)}, f32[1,6,384]{2,1,0:T(8,128)S(1)}, f32[1536]{0:T(1024)S(1)}) all-reduce(f32[384]{0:T(512)S(1)} %reduce_sum.220, f32[384]{0:T(512)S(1)} %reduce_sum.222, bf16[1,6,384]{2,1,0:T(8,128)(2,1)S(1)} %copy.61, ...), channel_id=1, replica_groups=mesh['dp'=16,'tensor'=2] {'dp'}, use_global_device_ids=true, to_apply=%region_18.19 | all-reduce | flops 4608 | bytes 32256 | tf_op jit(solution)/shard_map/psum | solution.py:199
  478.5 290.0 %all-reduce.4.cloned.1.call-done = (f32[768,384]{1,0:T(8,128)}, f32[768,384]{1,0:T(8,128)}, f32[768,384]{1,0:T(8,128)}, f32[384,768]{1,0:T(8,128)}, f32[768,1536]{1,0:T(8,128)}, /*index=5*/f32[1536,768]{1,0:T(8,128)}) async-done(((f32[768,384]{1,0:T(8,128)}, f32[768,384]{1,0:T(8,128)}, f32[768,384]{1,0:T(8,128)}, f32[384,768]{1,0:T(8,128)}, f32[768,1536]{1,0:T(8,128)}, /*index=5*/f32[1536,768]{1,0:T(8,128)}), ...) | async-done | bytes 14155792 | tf_op jit(solution)/shard_map/psum | solution.py:199
  773.3 2.9 broadcast_multiply_fusion.1
  (209 shorter events, 69.4 us)
Async XLA Ops:
  7.2 110.5 %copy-start = (bf16[768,1536]{1,0:T(8,128)(2,1)S(1)}, bf16[768,1536]{1,0:T(8,128)(2,1)}, u32[]{:S(2)}) copy-start(bf16[768,1536]{1,0:T(8,128)(2,1)} %param.31) | copy-start | bytes 7077892
  7.2 32.9 %copy-start.38 = (bf16[384]{0:T(512)(128)(2,1)S(1)}, bf16[384]{0:T(512)(128)(2,1)}, u32[]{:S(2)}) copy-start(bf16[384]{0:T(512)(128)(2,1)} %param.23) | copy-start | bytes 2308
  7.2 32.9 %copy-start.39 = (bf16[384]{0:T(512)(128)(2,1)S(1)}, bf16[384]{0:T(512)(128)(2,1)}, u32[]{:S(2)}) copy-start(bf16[384]{0:T(512)(128)(2,1)} %param.26) | copy-start | bytes 2308
  7.2 32.9 %copy-start.2 = (s32[16]{0:T(128)S(1)}, s32[16]{0:T(128)}, u32[]{:S(2)}) copy-start(s32[16]{0:T(128)} %param.20) | copy-start | bytes 196
  7.2 40.4 %all-gather.6.cloned.1.call-start = ((), (), s32[]{:S(2)}) async-start(), calls=%async_computation.7 | async-start | bytes 2359296 | tf_op jit(solution)/shard_map/all_gather | solution.py:93
  40.0 10.2 %copy-start.31 = (bf16[768,384]{1,0:T(8,128)(2,1)S(1)}, bf16[768,384]{1,0:T(8,128)(2,1)}, u32[]{:S(2)}) copy-start(bf16[768,384]{1,0:T(8,128)(2,1)} %param.22) | copy-start | bytes 1769476
  40.0 62.2 %reduce-scatter.10.cloned.1.call-start = ((), (), s32[]{:S(2)}) async-start(), calls=%async_computation.8 | async-start | bytes 4718592 | tf_op jit(solution)/shard_map/reduce_scatter | solution.py:120
  50.2 11.5 %copy-start.15 = (bf16[1024,384]{0,1:T(8,128)(2,1)}, bf16[1024,384]{0,1:T(8,128)(2,1)S(1)}, u32[]{:S(2)}) copy-start(bf16[1024,384]{0,1:T(8,128)(2,1)S(1)} %fusion.79) | copy-start | bytes 2359300
  51.0 10.6 %copy-start.17 = (bf16[1024,384]{0,1:T(8,128)(2,1)}, bf16[1024,384]{0,1:T(8,128)(2,1)S(1)}, u32[]{:S(2)}) copy-start(bf16[1024,384]{0,1:T(8,128)(2,1)S(1)} %add_convert_fusion.1) | copy-start | bytes 2359300
  61.6 11.8 %copy-start.33 = (bf16[768,384]{1,0:T(8,128)(2,1)S(1)}, bf16[768,384]{1,0:T(8,128)(2,1)}, u32[]{:S(2)}) copy-start(bf16[768,384]{1,0:T(8,128)(2,1)} %param.25) | copy-start | bytes 1769476
  74.2 11.9 %copy-start.13 = (bf16[1024,384]{0,1:T(8,128)(2,1)}, bf16[1024,384]{0,1:T(8,128)(2,1)S(1)}, u32[]{:S(2)}) copy-start(bf16[1024,384]{0,1:T(8,128)(2,1)S(1)} %add_convert_fusion.2) | copy-start | bytes 2359300
  74.3 12.7 %copy-start.29 = (bf16[384,768]{1,0:T(8,128)(2,1)S(1)}, bf16[384,768]{1,0:T(8,128)(2,1)}, u32[]{:S(2)}) copy-start(bf16[384,768]{1,0:T(8,128)(2,1)} %param.27) | copy-start | bytes 1769476
  89.8 28.0 %all-gather.8.cloned.1.call-start = ((), (), s32[]{:S(2)}) async-start(), calls=%async_computation.9 | async-start | bytes 2359296 | tf_op jit(solution)/shard_map/all_gather | solution.py:126
  106.5 47.9 %reduce-scatter.12.cloned.1.call-start = ((), (), s32[]{:S(2)}) async-start(), calls=%async_computation.10 | async-start | bytes 4718592 | tf_op jit(solution)/shard_map/reduce_scatter | solution.py:132
  117.7 19.9 %copy-start.47 = (bf16[1536,768]{1,0:T(8,128)(2,1)S(1)}, bf16[1536,768]{1,0:T(8,128)(2,1)}, u32[]{:S(2)}) copy-start(bf16[1536,768]{1,0:T(8,128)(2,1)} %param.33) | copy-start | bytes 7077892
  141.9 31.2 %all-gather.10.cloned.1.call-start = ((), (), s32[]{:S(2)}) async-start(), calls=%async_computation.11 | async-start | bytes 2359296 | tf_op jit(solution)/shard_map/all_gather | solution.py:140
  161.8 39.9 %reduce-scatter.14.cloned.1.call-start = ((), (), s32[]{:S(2)}) async-start(), calls=%async_computation.12 | async-start | bytes 4718592 | tf_op jit(solution)/shard_map/reduce_scatter | solution.py:149
  189.2 12.5 %copy-start.4 = (f32[1,512,768]{2,1,0:T(8,128)S(1)}, f32[1,512,768]{2,1,0:T(8,128)}, u32[]{:S(2)}) copy-start(f32[1,512,768]{2,1,0:T(8,128)} %copy-done.3) | copy-start | bytes 4718596
  189.3 29.3 %all-gather.12.cloned.1.call-start = ((), (), s32[]{:S(2)}) async-start(), calls=%async_computation.13 | async-start | bytes 2359296 | tf_op jit(solution)/shard_map/all_gather | solution.py:152
  204.5 14.1 %copy-start.30 = (bf16[384,768]{1,0:T(8,128)(2,1)S(1)}, bf16[384,768]{1,0:T(8,128)(2,1)}, u32[]{:S(2)}) copy-start(bf16[384,768]{1,0:T(8,128)(2,1)} %param.27) | copy-start | bytes 1769476
  206.3 14.6 %copy-start.14 = (bf16[1024,384]{0,1:T(8,128)(2,1)S(1)}, bf16[1024,384]{0,1:T(8,128)(2,1)}, u32[]{:S(2)}) copy-start(bf16[1024,384]{0,1:T(8,128)(2,1)} %copy-done.13) | copy-start | bytes 2359300
  207.4 144.8 %reduce-scatter.16.cloned.1.call-start = ((), (), s32[]{:S(2)}) async-start(), calls=%async_computation.14 | async-start | bytes 2359296
  231.1 12.4 %copy-start.18 = (bf16[1024,384]{0,1:T(8,128)(2,1)S(1)}, bf16[1024,384]{0,1:T(8,128)(2,1)}, u32[]{:S(2)}) copy-start(bf16[1024,384]{0,1:T(8,128)(2,1)} %copy-done.17) | copy-start | bytes 2359300
  243.4 34.2 %copy-start.16 = (bf16[1024,384]{0,1:T(8,128)(2,1)S(1)}, bf16[1024,384]{0,1:T(8,128)(2,1)}, u32[]{:S(2)}) copy-start(bf16[1024,384]{0,1:T(8,128)(2,1)} %copy-done.15) | copy-start | bytes 2359300
  277.6 34.3 %copy-start.23 = (bf16[6,64,1024]{2,1,0:T(8,128)(2,1)}, bf16[6,64,1024]{2,1,0:T(8,128)(2,1)S(1)}, u32[]{:S(2)}) copy-start(bf16[6,64,1024]{2,1,0:T(8,128)(2,1)S(1)} %fusion.88) | copy-start | bytes 2359300
  327.8 47.2 %reduce-scatter.18.cloned.1.call-start = ((), (), s32[]{:S(2)}) async-start(), calls=%async_computation.15 | async-start | bytes 294912
  328.0 7.4 copy-start.11
  328.0 7.4 copy-start.12
  335.4 5.9 copy-start.22
  341.0 427.5 %all-reduce.4.cloned.1.call-start = ((), (), s32[]{:S(2)}) async-start(), calls=%async_computation.16 | async-start | bytes 28311552 | tf_op jit(solution)/shard_map/psum | solution.py:199
  367.4 108.7 %all-to-all-start.1 = ((bf16[16,2,12288]{2,1,0:T(2,128)(2,1)}), bf16[16,2,12288]{2,1,0:T(2,128)(2,1)S(1)}, u32[]{:S(2)}, u32[]{:S(2)}) async-start(bf16[16,2,12288]{2,1,0:T(2,128)(2,1)} %reshape.457), calls=%async_computation.4 | async-start | bytes 1572864 | tf_op jit(solution)/shard_map/all_to_all | solution.py:194
  768.5 4.9 copy-start.9
  (30 other events, 74.6 us)
Sparse Core Ops, SparseCore 0:
  40.1 7.4 all-gather.5
  89.9 12.3 reduce-scatter.9
  106.6 11.0 all-gather.7
  142.0 12.3 reduce-scatter.11
  162.0 11.0 all-gather.9
  189.4 12.3 reduce-scatter.13
  207.5 11.0 all-gather.11
  327.9 10.2 reduce-scatter.15
  341.1 8.8 reduce-scatter.17
  357.4 411.0 all-reduce.3
where the time goes:
time: 798 us; the launch traced here: 789 us
  waiting for transfers between devices  364 us (46%)
  matrix products  186 us (23%)
  blocking collectives  130 us (16%)
  other arithmetic  46.5 us (6%)
  local copies, waits for them, and re-layouts  39.5 us (5%)
  between operations  15.4 us (2%)
    psum x1, waiting for transfers between devices, on_device(): lax.psum((grad_w_query, grad_b_query, grad_w_key, grad_w_value, grad_b_va...  290 us
    dot_general x24, matrix products, product(): return jnp.einsum(form, left, right, preferred_element_type=jnp.float32)  186 us
    psum x1, blocking collectives, on_device(): lax.psum((grad_w_query, grad_b_query, grad_w_key, grad_w_value, grad_b_va...  98 us
    all_to_all x1, blocking collectives, on_device(): lax.all_to_all(arranged, 'dp', split_axis=0, concat_axis=1, tiled=True)  29.5 us
    unnamed x114, local copies, waits for them, and re-layouts  28.1 us
  transfers between devices with their start and end apart: 11, of which 8 were waited for; matrix products, arithmetic and copies ran while one was open for 6% of the time, Pallas kernels for 0%

commit v1 on v0

--- a/solution.py
+++ b/solution.py
@@ -6,6 +6,20 @@
 HEAD_DIM = 64
 epsilon = 1e-06
 masked_score = -1e30
+
+
+def recover_the_entries(panel, out_dim, vals):
+    arr_now = panel.shape
+    y2 = panel.reshape(*arr_now[:out_dim], vals, arr_now[out_dim] // vals, *arr_now[out_dim + 1 :])
+    part_next = jnp.moveaxis(y2, out_dim, 0)
+    return part_next
+
+
+def unite_the_axis_part(payload, along_dim):
+    m_next = list(payload.shape[1:])
+    m_next[along_dim] *= payload.shape[0]
+    u_next = jnp.moveaxis(payload, 0, along_dim).reshape(m_next)
+    return u_next
 
 
 def layer_norm(value, gain, shift):
@@ -88,7 +102,15 @@
     factor = (order.shape[0] * seq_len) ** (-0.5)
     arranged = inputs[order]
     vectors = jnp.stack([b_out, gain_one, shift_one, b_down, gain_two, shift_two])[None]
-    dealt_half = lax.all_to_all(arranged, "dp", split_axis=0, concat_axis=1, tiled=True)
+    formed, near = (lax.axis_size("dp"), lax.axis_index("dp"))
+    low = recover_the_entries(arranged, 0, formed)
+    d_next = low
+    for dd in range(1, formed):
+        current_value, next_value = ((near + dd) % formed, (near - dd) % formed)
+        after = lax.dynamic_index_in_dim(low, current_value, 0)
+        s_next = lax.ppermute(after, "dp", perm=[(u, (u + dd) % formed) for u in range(formed)])
+        d_next = lax.dynamic_update_slice_in_dim(d_next, s_next, next_value, axis=0)
+    dealt_half = unite_the_axis_part(d_next, 1)
     dealt, vectors_full = (
         lax.all_gather(dealt_half, "tensor", axis=2, tiled=True),
         lax.all_gather(vectors, "tensor", axis=2, tiled=True),

time: 798 us -> 845 us (1.059)
  waiting for transfers between devices: 364 us -> 407 us
  starting transfers between devices: 7.87 us -> 40.7 us
  blocking collectives: 130 us -> 100 us
    ppermute x0 -> x15, waiting for transfers between devices: none -> 39.7 us  [on_device(): lax.ppermute(after, 'dp', perm=[(u, (u + dd) % formed) for u in range(for...]
    ppermute x0 -> x15, starting transfers between devices: none -> 32.6 us  [on_device(): lax.ppermute(after, 'dp', perm=[(u, (u + dd) % formed) for u in range(for...]
    all_to_all x1 -> x0, blocking collectives: 29.5 us -> none  [on_device(): lax.all_to_all(arranged, 'dp', split_axis=0, concat_axis=1, tiled=True)]
    unnamed x114 -> x116, local copies, waits for them, and re-layouts: 28.1 us -> 29 us
  transfers between devices with their start and end apart: 11 -> 26, of which waited for: 8 -> 18; matrix products, arithmetic and copies ran while one was open for 6% -> 6% of each run, Pallas kernels for 0% -> 0%
where the time goes in v1:
time: 845 us; the launch traced here: 842 us
  waiting for transfers between devices  407 us (48%)
  matrix products  187 us (22%)
  blocking collectives  100 us (12%)
  other arithmetic  46.4 us (5%)
  local copies, waits for them, and re-layouts  45.4 us (5%)
  starting transfers between devices  40.7 us (5%)
  between operations  15.7 us (2%)
    psum x1, waiting for transfers between devices, on_device(): lax.psum((grad_w_query, grad_b_query, grad_w_key, grad_w_value, grad_b_va...  290 us
    dot_general x24, matrix products, product(): return jnp.einsum(form, left, right, preferred_element_type=jnp.float32)  187 us
    psum x1, blocking collectives, on_device(): lax.psum((grad_w_query, grad_b_query, grad_w_key, grad_w_value, grad_b_va...  98.4 us
    ppermute x15, waiting for transfers between devices, on_device(): lax.ppermute(after, 'dp', perm=[(u, (u + dd) % formed) for u in range(for...  39.7 us
    ppermute x15, starting transfers between devices, on_device(): lax.ppermute(after, 'dp', perm=[(u, (u + dd) % formed) for u in range(for...  32.6 us
    unnamed x116, local copies, waits for them, and re-layouts  29 us
  transfers between devices with their start and end apart: 26, of which 18 were waited for; matrix products, arithmetic and copies ran while one was open for 6% of the time, Pallas kernels for 0%

profile of v1, /device:TPU:0, one launch (start us, length us, event | category | flops | bytes accessed | tf_op | source)
XLA Modules:
  0.0 841.6 jit_solution(6224944460485143574)
XLA Ops:
  23.1 5.1 collective-permute-done.1
  28.2 7.0 collective-permute-done.2
  35.2 6.1 collective-permute-done.3
  43.2 5.1 collective-permute-done.4
  49.9 4.5 collective-permute-done.5
  72.7 4.2 collective-permute-start.9
  91.1 8.5 %all-gather.6.cloned.1.call-done = bf16[1,1024,768]{2,1,0:T(8,128)(2,1)} async-done(((bf16[1,1024,384]{2,1,0:T(8,128)(2,1)}), bf16[1,1024,768]{2,1,0:T(8,128)(2,1)}) %all-gather.6.cloned.1.call-update) | async-done | bytes 1572880 | tf_op jit(solution)/shard_map/all_gather | solution.py:115
  102.9 10.6 %fusion.3 = (f32[6,1024]{1,0:T(8,128)S(1)}, f32[6,1024,1024]{1,2,0:T(8,128)}) fusion(pred[1024]{0:T(1024)(128)(4,1)S(1)} %iota_compare_fusion, bf16[1024,6,64]{0,2,1:T(8,128)(2,1)S(1)} %bitcast.172, bf16[1024,6,64]{0,2,1:T(8,128)(2,1)S(1)} %bitcast.170), kind=kOutput, calls=%fused_computation.13 | convolution fusion | flops 824174592 | bytes 26764288 | tf_op jit(solution)/shard_map/while/body/eval_jaxpr/qhd,khd->hqk/dot_general | solution.py:36
  113.5 11.8 %fusion.2 = f32[6,1024]{1,0:T(8,128)S(1)} fusion(f32[6,1024,1024]{1,2,0:T(8,128)} %get-tuple-element.127, f32[6,1024]{1,0:T(8,128)S(1)} %get-tuple-element.126, pred[1024]{0:T(1024)(128)(4,1)S(1)} %iota_compare_fusion), kind=kLoop, calls=%fused_computation.12 | loop fusion | flops 25159680 | bytes 25216000 | tf_op jit(solution)/shard_map/while/body/eval_jaxpr/reduce_sum | solution.py:51
  126.1 11.9 %fusion.91 = bf16[6,64,1024]{2,1,0:T(8,128)(2,1)S(1)} fusion(bf16[1024,6,64]{0,2,1:T(8,128)(2,1)S(1)} %bitcast.166, f32[6,1024,1024]{1,2,0:T(8,128)} %get-tuple-element.127, f32[6,1024]{1,0:T(8,128)S(1)} %fusion.2, f32[6,1024]{1,0:T(8,128)S(1)} %get-tuple-element.126, pred[1024]{0:T(1024)(128)(4,1)S(1)} %iota_compare_fusion), kind=kOutput, calls=%fused_computation.106 | convolution fusion | flops 837156864 | bytes 26788864 | tf_op jit(solution)/shard_map/while/body/eval_jaxpr/hqk,khd->qhd/dot_general | solution.py:36
  143.8 10.4 %reduce-scatter.10.cloned.1.call-done = f32[1,512,768]{2,1,0:T(8,128)} async-done(((f32[1,1024,768]{2,1,0:T(8,128)}), f32[1,512,768]{2,1,0:T(8,128)}) %reduce-scatter.10.cloned.1.call-update) | async-done | bytes 1572880 | tf_op jit(solution)/shard_map/reduce_scatter | solution.py:142
  159.0 10.7 %all-gather.8.cloned.1.call-done = bf16[1,1024,768]{2,1,0:T(8,128)(2,1)} async-done(((bf16[1,512,768]{2,1,0:T(8,128)(2,1)}), bf16[1,1024,768]{2,1,0:T(8,128)(2,1)}) %all-gather.8.cloned.1.call-update) | async-done | bytes 1572880 | tf_op jit(solution)/shard_map/all_gather | solution.py:148
  169.7 18.2 %multiply_convert_fusion.1 = (bf16[1024,1536]{1,0:T(8,128)(2,1)S(1)}, f32[1024,1536]{1,0:T(8,128)}, f32[1024,1536]{1,0:T(8,128)}) fusion(f32[1536]{0:T(1024)S(1)} %convert_element_type.127, bf16[768,1536]{1,0:T(8,128)(2,1)S(1)} %copy-done, bf16[1,1024,768]{2,1,0:T(8,128)(2,1)} %all-gather.8.cloned.1.call-done), kind=kOutput, calls=%fused_computation.31 | convolution fusion | flops 2519728128 | bytes 19666944 | tf_op jit(solution)/shard_map/nd,df->nf/dot_general | solution.py:36
  189.5 4.3 convolution_bitcast_fusion.1
  193.8 12.4 %reduce-scatter.12.cloned.1.call-done = f32[1,512,768]{2,1,0:T(8,128)} async-done(((f32[1,1024,768]{2,1,0:T(8,128)}), f32[1,512,768]{2,1,0:T(8,128)}) %reduce-scatter.12.cloned.1.call-update) | async-done | bytes 1572880 | tf_op jit(solution)/shard_map/reduce_scatter | solution.py:154
  213.8 11.2 %all-gather.10.cloned.1.call-done = bf16[1,1024,768]{2,1,0:T(8,128)(2,1)} async-done(((bf16[1,512,768]{2,1,0:T(8,128)(2,1)}), bf16[1,1024,768]{2,1,0:T(8,128)(2,1)}) %all-gather.10.cloned.1.call-update) | async-done | bytes 1572880 | tf_op jit(solution)/shard_map/all_gather | solution.py:162
  225.0 10.2 %fusion.118 = (f32[1536]{0:T(1024)S(1)}, bf16[1024,1536]{1,0:T(8,128)(2,1)S(1)}) fusion(f32[1024,1536]{1,0:T(8,128)} %get-tuple-element.103, bf16[1536,768]{1,0:T(8,128)(2,1)} %param.33, bf16[1,1024,768]{2,1,0:T(8,128)(2,1)} %all-gather.10.cloned.1.call-done, f32[1024,1536]{1,0:T(8,128)} %get-tuple-element.128, f32[1536]{0:T(1024)S(1)} %convert_element_type.127), kind=kOutput, calls=%fused_computation.198 | convolution fusion | flops 2441083392 | bytes 19673088 | tf_op jit(solution)/shard_map/nd,fd->nf/dot_general | solution.py:36
  236.9 4.3 convolution_bitcast_fusion
  241.2 12.4 %reduce-scatter.14.cloned.1.call-done = f32[1,512,768]{2,1,0:T(8,128)} async-done(((f32[1,1024,768]{2,1,0:T(8,128)}), f32[1,512,768]{2,1,0:T(8,128)}) %reduce-scatter.14.cloned.1.call-update) | async-done | bytes 1572880 | tf_op jit(solution)/shard_map/reduce_scatter | solution.py:171
  259.4 11.2 %all-gather.12.cloned.1.call-done = bf16[1,1024,768]{2,1,0:T(8,128)(2,1)} async-done(((bf16[1,512,768]{2,1,0:T(8,128)(2,1)}), bf16[1,1024,768]{2,1,0:T(8,128)(2,1)}) %all-gather.12.cloned.1.call-update) | async-done | bytes 1572880 | tf_op jit(solution)/shard_map/all_gather | solution.py:174
  272.8 10.2 %fusion.119 = f32[6,1024,1024]{1,2,0:T(8,128)} fusion(bf16[1024,6,64]{0,2,1:T(8,128)(2,1)S(1)} %bitcast.168, bf16[1024,6,64]{0,2,1:T(8,128)(2,1)S(1)} %bitcast.167), kind=kOutput, calls=%fused_computation.199 | convolution fusion | flops 805306368 | bytes 26738688 | tf_op jit(solution)/shard_map/while/body/eval_jaxpr/qhd,khd->hqk/dot_general | solution.py:36
  283.0 12.4 %convert_reduce_fusion = (f32[6,64]{1,0:T(8,128)S(1)}, bf16[6,64,1024]{2,1,0:T(8,128)(2,1)}) fusion(bf16[1024,6,64]{0,2,1:T(8,128)(2,1)S(1)} %bitcast.169, f32[6,1024,1024]{1,2,0:T(8,128)} %get-tuple-element.127, f32[6,1024]{1,0:T(8,128)S(1)} %log_add_fusion, pred[1024]{0:T(1024)(128)(4,1)S(1)} %iota_compare_fusion), kind=kOutput, calls=%fused_computation.88 | convolution fusion | flops 831651456 | bytes 26765824 | tf_op jit(solution)/shard_map/while/body/eval_jaxpr/hqk,qhd->khd/dot_general | solution.py:36
  295.4 34.1 %fusion.88 = bf16[6,64,1024]{2,1,0:T(8,128)(2,1)S(1)} fusion(bf16[1024,6,64]{0,2,1:T(8,128)(2,1)S(1)} %bitcast.173, f32[6,1024,1024]{1,2,0:T(8,128)} %fusion.119, f32[6,1024,1024]{1,2,0:T(8,128)} %get-tuple-element.127, f32[6,1024]{1,0:T(8,128)S(1)} %log_add_fusion, pred[1024]{0:T(1024)(128)(4,1)S(1)} %iota_compare_fusion), kind=kOutput, calls=%fused_computation.105 | convolution fusion | flops 874912768 | bytes 51930112 | tf_op jit(solution)/shard_map/while/body/eval_jaxpr/hqk,qhd->khd/dot_general | solution.py:36
  329.6 34.2 %convert_reduce_fusion.1 = (f32[6,64]{1,0:T(8,128)S(1)}, bf16[6,64,1024]{2,1,0:T(8,128)(2,1)S(1)}) fusion(bf16[1024,6,64]{0,2,1:T(8,128)(2,1)S(1)} %bitcast.171, f32[6,1024,1024]{1,2,0:T(8,128)} %fusion.119, f32[6,1024,1024]{1,2,0:T(8,128)} %get-tuple-element.127, f32[6,1024]{1,0:T(8,128)S(1)} %log_add_fusion, pred[1024]{0:T(1024)(128)(4,1)S(1)} %iota_compare_fusion), kind=kOutput, calls=%fused_computation.89 | convolution fusion | flops 875698816 | bytes 51931648 | tf_op jit(solution)/shard_map/while/body/eval_jaxpr/hqk,khd->qhd/dot_general | solution.py:36
  370.4 5.6 copy.58
  380.0 7.4 fusion.48
  387.3 4.3 fusion.54
  407.3 5.0 copy.53
  412.8 5.4 reduce.43
  419.3 6.8 all-to-all-start
  428.2 98.4 %all-reduce = (f32[384]{0:T(512)S(1)}, f32[384]{0:T(512)S(1)}, f32[1,6,384]{2,1,0:T(8,128)S(1)}, f32[1536]{0:T(1024)S(1)}) all-reduce(f32[384]{0:T(512)S(1)} %reduce_sum.220, f32[384]{0:T(512)S(1)} %reduce_sum.222, bf16[1,6,384]{2,1,0:T(8,128)(2,1)S(1)} %copy.61, ...), channel_id=1, replica_groups=mesh['dp'=16,'tensor'=2] {'dp'}, use_global_device_ids=true, to_apply=%region_18.19 | all-reduce | flops 4608 | bytes 32256 | tf_op jit(solution)/shard_map/psum | solution.py:221
  530.9 289.8 %all-reduce.4.cloned.1.call-done = (f32[768,384]{1,0:T(8,128)}, f32[768,384]{1,0:T(8,128)}, f32[768,384]{1,0:T(8,128)}, f32[384,768]{1,0:T(8,128)}, f32[768,1536]{1,0:T(8,128)}, /*index=5*/f32[1536,768]{1,0:T(8,128)}) async-done(((f32[768,384]{1,0:T(8,128)}, f32[768,384]{1,0:T(8,128)}, f32[768,384]{1,0:T(8,128)}, f32[384,768]{1,0:T(8,128)}, f32[768,1536]{1,0:T(8,128)}, /*index=5*/f32[1536,768]{1,0:T(8,128)}), ...) | async-done | bytes 14155792 | tf_op jit(solution)/shard_map/psum | solution.py:221
  (256 shorter events, 132.0 us)
Async XLA Ops:
  7.2 162.5 %copy-start = (bf16[768,1536]{1,0:T(8,128)(2,1)S(1)}, bf16[768,1536]{1,0:T(8,128)(2,1)}, u32[]{:S(2)}) copy-start(bf16[768,1536]{1,0:T(8,128)(2,1)} %param.31) | copy-start | bytes 7077892
  7.2 81.9 %copy-start.39 = (bf16[384]{0:T(512)(128)(2,1)S(1)}, bf16[384]{0:T(512)(128)(2,1)}, u32[]{:S(2)}) copy-start(bf16[384]{0:T(512)(128)(2,1)} %param.23) | copy-start | bytes 2308
  7.2 81.9 %copy-start.40 = (bf16[384]{0:T(512)(128)(2,1)S(1)}, bf16[384]{0:T(512)(128)(2,1)}, u32[]{:S(2)}) copy-start(bf16[384]{0:T(512)(128)(2,1)} %param.26) | copy-start | bytes 2308
  7.2 81.9 %copy-start.2 = (s32[16]{0:T(128)S(1)}, s32[16]{0:T(128)}, u32[]{:S(2)}) copy-start(s32[16]{0:T(128)} %param.20) | copy-start | bytes 196
  7.2 92.3 %all-gather.6.cloned.1.call-start = ((), (), s32[]{:S(2)}) async-start(), calls=%async_computation.6 | async-start | bytes 2359296 | tf_op jit(solution)/shard_map/all_gather | solution.py:115
  11.3 9.9 %collective-permute-start = (bf16[1,1,64,384]{3,2,0,1:T(8,128)(2,1)}, bf16[1,1,64,384]{3,2,0,1:T(8,128)(2,1)}, u32[]{:S(2)}, u32[]{:S(2)}) collective-permute-start(bf16[1,1,64,384]{3,2,0,1:T(8,128)(2,1)} %get-tuple-element.125), channel_id=1, source_target_pairs={{0,2},{2,4},{4,6},{6,8},{8,10},{10,12},{12,14},{14,16},{16,18},{18... | collective-permute-start | bytes 147464 | tf_op jit(solution)/shard_map/ppermute | solution.py:111
  14.3 72.8 %collective-permute-start.14 = (bf16[1,1,64,384]{3,2,0,1:T(8,128)(2,1)S(1)}, bf16[1,1,64,384]{3,2,0,1:T(8,128)(2,1)}, u32[]{:S(2)}, u32[]{:S(2)}) collective-permute-start(bf16[1,1,64,384]{3,2,0,1:T(8,128)(2,1)S(1)} %get-tuple-element.111), channel_id=1, source_target_pairs={{0,30},{2,0},{4,2},{6,4},{8,6},{10,8},{12,10},{14,12},{16,14},{18,... | collective-permute-start | bytes 147464 | tf_op jit(solution)/shard_map/ppermute | solution.py:111
  18.3 68.0 %collective-permute-start.13 = (bf16[1,1,64,384]{3,2,0,1:T(8,128)(2,1)S(1)}, bf16[1,1,64,384]{3,2,0,1:T(8,128)(2,1)}, u32[]{:S(2)}, u32[]{:S(2)}) collective-permute-start(bf16[1,1,64,384]{3,2,0,1:T(8,128)(2,1)S(1)} %get-tuple-element.112), channel_id=1, source_target_pairs={{0,28},{2,30},{4,0},{6,2},{8,4},{10,6},{12,8},{14,10},{16,12},{18,... | collective-permute-start | bytes 147464 | tf_op jit(solution)/shard_map/ppermute | solution.py:111
  20.3 65.1 %collective-permute-start.12 = (bf16[1,1,64,384]{3,2,0,1:T(8,128)(2,1)S(1)}, bf16[1,1,64,384]{3,2,0,1:T(8,128)(2,1)}, u32[]{:S(2)}, u32[]{:S(2)}) collective-permute-start(bf16[1,1,64,384]{3,2,0,1:T(8,128)(2,1)S(1)} %get-tuple-element.113), channel_id=1, source_target_pairs={{0,26},{2,28},{4,30},{6,0},{8,2},{10,4},{12,6},{14,8},{16,10},{18,... | collective-permute-start | bytes 147464 | tf_op jit(solution)/shard_map/ppermute | solution.py:111
  20.8 63.8 %collective-permute-start.11 = (bf16[1,1,64,384]{3,2,0,1:T(8,128)(2,1)S(1)}, bf16[1,1,64,384]{3,2,0,1:T(8,128)(2,1)}, u32[]{:S(2)}, u32[]{:S(2)}) collective-permute-start(bf16[1,1,64,384]{3,2,0,1:T(8,128)(2,1)S(1)} %get-tuple-element.114), channel_id=1, source_target_pairs={{0,24},{2,26},{4,28},{6,30},{8,0},{10,2},{12,4},{14,6},{16,8},{18,... | collective-permute-start | bytes 147464 | tf_op jit(solution)/shard_map/ppermute | solution.py:111
  21.2 7.0 collective-permute-start.1
  28.2 7.0 collective-permute-start.2
  35.2 6.1 collective-permute-start.3
  41.3 7.0 collective-permute-start.4
  48.3 6.1 collective-permute-start.5
  54.4 6.1 collective-permute-start.6
  60.5 6.3 collective-permute-start.7
  66.8 5.9 collective-permute-start.8
  72.7 6.0 collective-permute-start.9
  78.7 5.9 collective-permute-start.10
  88.8 65.4 %reduce-scatter.10.cloned.1.call-start = ((), (), s32[]{:S(2)}) async-start(), calls=%async_computation.7 | async-start | bytes 4718592 | tf_op jit(solution)/shard_map/reduce_scatter | solution.py:142
  141.7 28.0 %all-gather.8.cloned.1.call-start = ((), (), s32[]{:S(2)}) async-start(), calls=%async_computation.8 | async-start | bytes 2359296 | tf_op jit(solution)/shard_map/all_gather | solution.py:148
  158.4 47.8 %reduce-scatter.12.cloned.1.call-start = ((), (), s32[]{:S(2)}) async-start(), calls=%async_computation.9 | async-start | bytes 4718592 | tf_op jit(solution)/shard_map/reduce_scatter | solution.py:154
  193.8 31.2 %all-gather.10.cloned.1.call-start = ((), (), s32[]{:S(2)}) async-start(), calls=%async_computation.10 | async-start | bytes 2359296 | tf_op jit(solution)/shard_map/all_gather | solution.py:162
  213.8 39.9 %reduce-scatter.14.cloned.1.call-start = ((), (), s32[]{:S(2)}) async-start(), calls=%async_computation.11 | async-start | bytes 4718592 | tf_op jit(solution)/shard_map/reduce_scatter | solution.py:171
  241.2 29.4 %all-gather.12.cloned.1.call-start = ((), (), s32[]{:S(2)}) async-start(), calls=%async_computation.12 | async-start | bytes 2359296 | tf_op jit(solution)/shard_map/all_gather | solution.py:174
  259.3 144.9 %reduce-scatter.16.cloned.1.call-start = ((), (), s32[]{:S(2)}) async-start(), calls=%async_computation.13 | async-start | bytes 2359296
  295.4 34.2 %copy-start.17 = (bf16[1024,384]{0,1:T(8,128)(2,1)S(1)}, bf16[1024,384]{0,1:T(8,128)(2,1)}, u32[]{:S(2)}) copy-start(bf16[1024,384]{0,1:T(8,128)(2,1)} %copy-done.16) | copy-start | bytes 2359300
  329.5 34.3 %copy-start.24 = (bf16[6,64,1024]{2,1,0:T(8,128)(2,1)}, bf16[6,64,1024]{2,1,0:T(8,128)(2,1)S(1)}, u32[]{:S(2)}) copy-start(bf16[6,64,1024]{2,1,0:T(8,128)(2,1)S(1)} %fusion.88) | copy-start | bytes 2359300
  379.7 47.2 %reduce-scatter.18.cloned.1.call-start = ((), (), s32[]{:S(2)}) async-start(), calls=%async_computation.14 | async-start | bytes 294912
  392.9 427.8 %all-reduce.4.cloned.1.call-start = ((), (), s32[]{:S(2)}) async-start(), calls=%async_computation.15 | async-start | bytes 28311552 | tf_op jit(solution)/shard_map/psum | solution.py:221
  419.3 109.1 %all-to-all-start = ((bf16[16,2,12288]{2,1,0:T(2,128)(2,1)}), bf16[16,2,12288]{2,1,0:T(2,128)(2,1)S(1)}, u32[]{:S(2)}, u32[]{:S(2)}) async-start(bf16[16,2,12288]{2,1,0:T(2,128)(2,1)} %reshape.473), calls=%async_computation.3 | async-start | bytes 1572864 | tf_op jit(solution)/shard_map/all_to_all | solution.py:216
  (46 other events, 246.7 us)
Sparse Core Ops, SparseCore 0:
  88.9 10.5 all-gather.5
  141.8 12.3 reduce-scatter.9
  158.5 11.0 all-gather.7
  193.9 12.3 reduce-scatter.11
  213.9 11.0 all-gather.9
  241.3 12.3 reduce-scatter.13
  259.4 11.0 all-gather.11
  379.8 10.2 reduce-scatter.15
  393.0 8.7 reduce-scatter.17
  409.3 411.3 all-reduce.3
